TPU v7x, 32 devices: a whole 2x2x4 slice. The times are simulated.
32 devices in a mesh: dp: 8 (over z, y), mp: 4 (over x, core).
Axes of the slice: x: 2, y: 2, z: 4, core: 2. Of those that a mesh axis runs over, the one named last changes fastest.
Arguments:
- tokens: bfloat16 [16384, 1024], P(('dp', 'mp')), may hold values from -6 to 6
- segment_ids: int32 [16384], P(('dp', 'mp')), may hold values from 0 to 63, never falling along the last dimension, each value on 1 to 512 neighbouring positions
- w_qkv: bfloat16 [3, 1024, 1024], P(None, None, 'mp'), may hold values from -0.1875 to 0.1875
- b_qv: bfloat16 [2, 1024], P(None, 'mp'), may hold values from -1.75 to 1.75
- w_out: bfloat16 [1024, 1024], P('mp'), may hold values from -2 to 2
- b_out: bfloat16 [1024], replicated, may hold values from -1.75 to 1.75
- w_up: bfloat16 [1024, 4096], P(None, 'mp'), may hold values from -0.1875 to 0.1875
- b_up: bfloat16 [4096], P('mp'), may hold values from -1.75 to 1.75
- w_down: bfloat16 [4096, 1024], P('mp'), may hold values from -0.125 to 0.125
- b_down: bfloat16 [1024], replicated, may hold values from -1.75 to 1.75
- ln_gain: float32 [2, 1024], replicated, may hold values from 0.5 to 1.5
- ln_bias: float32 [2, 1024], replicated, may hold values from -1.75 to 1.75
- out_grad: bfloat16 [16384, 1024], P(('dp', 'mp')), may hold values from -6 to 6
Outputs:
- block_out: bfloat16 [16384, 1024], P(('dp', 'mp'))
- grad_in: float32 [16384, 1024], P(('dp', 'mp'))
- grad_qkv: float32 [3, 1024, 1024], P(None, None, 'mp')
- grad_bqv: float32 [2, 1024], P(None, 'mp')
- grad_wout: float32 [1024, 1024], P('mp')
- grad_bout: float32 [1024], replicated
- grad_up: float32 [1024, 4096], P(None, 'mp')
- grad_bup: float32 [4096], P('mp')
- grad_down: float32 [4096, 1024], P('mp')
- grad_bdown: float32 [1024], replicated
- grad_gain: float32 [2, 1024], replicated
- grad_shift: float32 [2, 1024], replicated
Inputs may be any that keep to these rules, and one draw needn't show every extreme that they name: `segment_ids`: along all frames in order, segment numbers never fall; each segment covers 1 to 512 frames and one covers exactly 512; attention never crosses a row of 1024 frames.
All inputs are finite; a program needn't handle non-finite values.
Results may differ from a plain program's by a relative error of at most 0.02.
Values may be sent and summed in bfloat16 or wider, within the bound.
No kernel may reach another device: no remote copies, remote signals or barrier semaphores. Data moves between devices by JAX's collectives and lax.ppermute only.
A program may use at most 192 MiB of HBM per device.

v0:
```python
import jax
import jax.numpy as jnp
from jax import lax
from jax.sharding import PartitionSpec as P

HD = 64
LEN = 1024
QBLK = 512


EPS = 1e-05


def norm_rows(values, gain, shift):
    center = values - jnp.mean(values, axis=-1, keepdims=True)
    spread = jnp.mean(center * center, axis=-1, keepdims=True)
    return center * lax.rsqrt(spread + EPS) * gain + shift


def split_heads(flat, rows):
    return flat.reshape(rows, LEN, flat.shape[1] // HD, HD)


def block_scores(query, keys, seg_q, seg_k, offset):
    scores = jnp.einsum(
        "rqhd,rkhd->rhqk", query, keys, preferred_element_type=jnp.float32
    ) * HD ** (-0.5)
    q_pos = offset + jnp.arange(query.shape[1], dtype=jnp.int32)
    k_pos = jnp.arange(keys.shape[1], dtype=jnp.int32)
    allowed = (seg_q[:, :, None] == seg_k[:, None, :]) & (
        k_pos[None, None, :] <= q_pos[None, :, None]
    )
    return jnp.where(allowed[:, None], scores, -1e30)


def attention_forward(query, keys, values, seg_all):
    rows = query.shape[0] // LEN
    q4 = split_heads(query, rows)
    k4 = split_heads(keys, rows)
    v4 = split_heads(values, rows)
    seg2 = seg_all.reshape(rows, LEN)
    outputs = []
    totals = []
    for block in range(LEN // QBLK):
        first = block * QBLK
        end = first + QBLK
        scores = block_scores(
            q4[:, first:end], k4[:, :end], seg2[:, first:end], seg2[:, :end], first
        )
        top = jnp.max(scores, axis=-1, keepdims=True)
        expd = jnp.exp(scores - top)
        summed = jnp.sum(expd, axis=-1, keepdims=True)
        weights = (expd / summed).astype(jnp.bfloat16)
        outputs.append(
            jnp.einsum("rhqk,rkhd->rqhd", weights, v4[:, :end], preferred_element_type=jnp.float32)
        )
        totals.append(top + jnp.log(summed))
    attended = jnp.concatenate(outputs, axis=1).reshape(query.shape).astype(jnp.bfloat16)
    return (attended, totals)


def attention_backward(query, keys, values, seg_all, totals, grad_att):
    rows = query.shape[0] // LEN
    q4 = split_heads(query, rows)
    k4 = split_heads(keys, rows)
    v4 = split_heads(values, rows)
    g4 = split_heads(grad_att, rows)
    seg2 = seg_all.reshape(rows, LEN)
    scale = HD ** (-0.5)
    grad_k = jnp.zeros(k4.shape, jnp.float32)
    grad_v = jnp.zeros(v4.shape, jnp.float32)
    grad_q_parts = []
    for block in range(LEN // QBLK):
        first = block * QBLK
        end = first + QBLK
        scores = block_scores(
            q4[:, first:end], k4[:, :end], seg2[:, first:end], seg2[:, :end], first
        )
        probs = jnp.exp(scores - totals[block])
        weights = probs.astype(jnp.bfloat16)
        grad_w = jnp.einsum(
            "rqhd,rkhd->rhqk", g4[:, first:end], v4[:, :end], preferred_element_type=jnp.float32
        )
        delta = jnp.sum(probs * grad_w, axis=-1, keepdims=True)
        grad_s = (probs * (grad_w - delta)).astype(jnp.bfloat16)
        grad_q_parts.append(
            jnp.einsum("rhqk,rkhd->rqhd", grad_s, k4[:, :end], preferred_element_type=jnp.float32)
            * scale
        )
        padding = ((0, 0), (0, LEN - end), (0, 0), (0, 0))
        grad_k = grad_k + jnp.pad(
            jnp.einsum(
                "rhqk,rqhd->rkhd", grad_s, q4[:, first:end], preferred_element_type=jnp.float32
            )
            * scale,
            padding,
        )
        grad_v = grad_v + jnp.pad(
            jnp.einsum(
                "rhqk,rqhd->rkhd", weights, g4[:, first:end], preferred_element_type=jnp.float32
            ),
            padding,
        )
    shape = query.shape
    grad_q = jnp.concatenate(grad_q_parts, axis=1).reshape(shape).astype(jnp.bfloat16)
    return (
        grad_q,
        grad_k.reshape(shape).astype(jnp.bfloat16),
        grad_v.reshape(shape).astype(jnp.bfloat16),
    )


def shards(
    tokens,
    segment_ids,
    w_qkv,
    b_qv,
    w_out,
    b_out,
    w_up,
    b_up,
    w_down,
    b_down,
    ln_gain,
    ln_bias,
    out_grad,
):
    resid = tokens.astype(jnp.float32)
    qv_bias = b_qv.astype(jnp.float32)
    up_bias = b_up.astype(jnp.float32)
    local_rows = tokens.shape[0]
    normed, first_back = jax.vjp(norm_rows, resid, ln_gain[0], ln_bias[0])
    lowered = normed.astype(jnp.bfloat16)
    joined, seg_all = (
        lax.all_gather(lowered, "mp", axis=0, tiled=True),
        lax.all_gather(segment_ids, "mp", axis=0, tiled=True),
    )
    query = (jnp.dot(joined, w_qkv[0], preferred_element_type=jnp.float32) + qv_bias[0]).astype(
        jnp.bfloat16
    )
    keys = jnp.dot(joined, w_qkv[1], preferred_element_type=jnp.float32).astype(jnp.bfloat16)
    values = (jnp.dot(joined, w_qkv[2], preferred_element_type=jnp.float32) + qv_bias[1]).astype(
        jnp.bfloat16
    )
    query, keys, values = (query, keys, values)
    attended, totals = attention_forward(query, keys, values, seg_all)
    attn_sum = lax.psum_scatter(
        jnp.dot(attended, w_out, preferred_element_type=jnp.float32).astype(jnp.bfloat16),
        "mp",
        scatter_dimension=0,
        tiled=True,
    ).astype(jnp.float32)
    mixed = resid + attn_sum + b_out.astype(jnp.float32)
    normed2, second_back = jax.vjp(norm_rows, mixed, ln_gain[1], ln_bias[1])
    lowered2 = normed2.astype(jnp.bfloat16)
    joined2 = lax.all_gather(lowered2, "mp", axis=0, tiled=True)
    pre_act = jnp.dot(joined2, w_up, preferred_element_type=jnp.float32) + up_bias
    pre_act, activ = (pre_act, jax.nn.gelu(pre_act, approximate=False).astype(jnp.bfloat16))
    block_out = (
        mixed
        + lax.psum_scatter(
            jnp.dot(activ, w_down, preferred_element_type=jnp.float32).astype(jnp.bfloat16),
            "mp",
            scatter_dimension=0,
            tiled=True,
        ).astype(jnp.float32)
        + b_down.astype(jnp.float32)
    ).astype(jnp.bfloat16)
    grad_y = out_grad.astype(jnp.float32)
    grad_z = lax.all_gather(out_grad, "mp", axis=0, tiled=True)
    grad_down = jnp.einsum("tf,td->fd", activ, grad_z, preferred_element_type=jnp.float32)
    grad_bdown = jnp.sum(grad_z, axis=0, dtype=jnp.float32)
    grad_act = jnp.einsum("td,fd->tf", grad_z, w_down, preferred_element_type=jnp.float32)
    gelu_back = jax.vjp(lambda value: jax.nn.gelu(value, approximate=False), pre_act)[1]
    grad_pre = gelu_back(grad_act)[0].astype(jnp.bfloat16)
    grad_up = jnp.einsum("td,tf->df", joined2, grad_pre, preferred_element_type=jnp.float32)
    grad_bup = jnp.sum(grad_pre, axis=0, dtype=jnp.float32)
    grad_n2 = lax.psum_scatter(
        jnp.einsum("tf,df->td", grad_pre, w_up, preferred_element_type=jnp.float32).astype(
            jnp.bfloat16
        ),
        "mp",
        scatter_dimension=0,
        tiled=True,
    ).astype(jnp.float32)
    grad_h, grad_g2, grad_s2 = second_back(grad_n2)
    grad_h = grad_h + grad_y
    grad_branch = lax.all_gather(grad_h.astype(jnp.bfloat16), "mp", axis=0, tiled=True)
    grad_wout = jnp.einsum("tc,td->cd", attended, grad_branch, preferred_element_type=jnp.float32)
    grad_bout = jnp.sum(grad_branch, axis=0, dtype=jnp.float32)
    grad_att = jnp.einsum(
        "td,cd->tc", grad_branch, w_out, preferred_element_type=jnp.float32
    ).astype(jnp.bfloat16)
    grad_q, grad_k, grad_v = attention_backward(query, keys, values, seg_all, totals, grad_att)
    grad_qkv = jnp.stack(
        [
            jnp.einsum("td,tc->dc", joined, piece, preferred_element_type=jnp.float32)
            for piece in (grad_q, grad_k, grad_v)
        ]
    )
    grad_bqv = jnp.stack(
        [jnp.sum(grad_q, axis=0, dtype=jnp.float32), jnp.sum(grad_v, axis=0, dtype=jnp.float32)]
    )
    summed = jnp.zeros((local_rows * lax.axis_size("mp"), w_qkv.shape[1]), jnp.float32)
    for index, piece in enumerate((grad_q, grad_k, grad_v)):
        summed = summed + jnp.einsum(
            "tc,dc->td", piece, w_qkv[index], preferred_element_type=jnp.float32
        )
    grad_n1 = lax.psum_scatter(
        summed.astype(jnp.bfloat16), "mp", scatter_dimension=0, tiled=True
    ).astype(jnp.float32)
    grad_x, grad_g1, grad_s1 = first_back(grad_n1)
    grad_in = grad_x + grad_h
    weight_totals = (
        lax.psum(grad_qkv.astype(jnp.bfloat16), "dp").astype(jnp.float32),
        lax.psum(grad_bqv.astype(jnp.bfloat16), "dp").astype(jnp.float32),
        lax.psum(grad_wout.astype(jnp.bfloat16), "dp").astype(jnp.float32),
        lax.psum(grad_bout.astype(jnp.bfloat16), "dp").astype(jnp.float32),
        lax.psum(grad_up.astype(jnp.bfloat16), "dp").astype(jnp.float32),
        lax.psum(grad_bup.astype(jnp.bfloat16), "dp").astype(jnp.float32),
        lax.psum(grad_down.astype(jnp.bfloat16), "dp").astype(jnp.float32),
        lax.psum(grad_bdown.astype(jnp.bfloat16), "dp").astype(jnp.float32),
    )
    norm_totals = lax.psum(
        (jnp.stack([grad_g1, grad_g2]), jnp.stack([grad_s1, grad_s2])), ("dp", "mp")
    )
    return (block_out, grad_in) + tuple(weight_totals) + tuple(norm_totals)


def solution(mesh):
    in_specs = (
        P(("dp", "mp"), None),
        P(("dp", "mp")),
        P(None, None, "mp"),
        P(None, "mp"),
        P("mp", None),
        P(),
        P(None, "mp"),
        P("mp"),
        P("mp", None),
        P(),
        P(),
        P(),
        P(("dp", "mp"), None),
    )
    out_specs = (
        P(("dp", "mp"), None),
        P(("dp", "mp"), None),
        P(None, None, "mp"),
        P(None, "mp"),
        P("mp", None),
        P(),
        P(None, "mp"),
        P("mp"),
        P("mp", None),
        P(),
        P(),
        P(),
    )
    return jax.shard_map(shards, mesh=mesh, in_specs=in_specs, out_specs=out_specs, check_vma=False)
```

profile of v0, /device:TPU:0, one launch (start us, length us, event | category | flops | bytes accessed | tf_op | source)
XLA Modules:
  0.0 795.6 jit_solution(3557118762227939732)
XLA Ops:
  15.4 6.2 all-gather
  25.2 27.5 %all-gather.6.cloned.1.call-done = bf16[2048,1024]{1,0:T(8,128)(2,1)} async-done(((bf16[512,1024]{1,0:T(8,128)(2,1)}), bf16[2048,1024]{1,0:T(8,128)(2,1)}) %all-gather.6.cloned.1.call-update) | async-done | bytes 4194320 | tf_op jit(solution)/shard_map/all_gather | solution.py:135
  52.7 3.6 fusion.22
  58.5 4.0 copy.62
  62.6 3.6 fusion.23
  100.5 4.0 fusion.55
  110.9 44.1 %reduce-scatter.5.cloned.1.call-done = bf16[512,1024]{1,0:T(8,128)(2,1)} async-done(((bf16[2048,1024]{1,0:T(8,128)(2,1)}), bf16[512,1024]{1,0:T(8,128)(2,1)}) %reduce-scatter.5.cloned.1.call-update) | async-done | bytes 1048592 | tf_op jit(solution)/shard_map/reduce_scatter | solution.py:147
  160.8 34.0 %all-gather.8.cloned.1.call-done = bf16[2048,1024]{1,0:T(8,128)(2,1)} async-done(((bf16[512,1024]{1,0:T(8,128)(2,1)}), bf16[2048,1024]{1,0:T(8,128)(2,1)}) %all-gather.8.cloned.1.call-update) | async-done | bytes 4194320 | tf_op jit(solution)/shard_map/all_gather | solution.py:156
  194.8 11.3 %fusion.91 = f32[2048,1024]{1,0:T(8,128)} fusion(bf16[2048,1024]{1,0:T(8,128)(2,1)} %all-gather.8.cloned.1.call-done, bf16[1024,1024]{1,0:T(8,128)(2,1)} %param.19), kind=kOutput, calls=%fused_computation.163 | convolution fusion | flops 4294967296 | bytes 14680064 | tf_op jit(solution)/shard_map/dot_general | solution.py:157
  206.1 24.6 %all-gather.10.cloned.1.call-done = bf16[2048,1024]{1,0:T(8,128)(2,1)} async-done(((bf16[512,1024]{1,0:T(8,128)(2,1)}), bf16[2048,1024]{1,0:T(8,128)(2,1)}) %all-gather.10.cloned.1.call-update) | async-done | bytes 4194320 | tf_op jit(solution)/shard_map/all_gather | solution.py:170
  230.7 27.2 %fusion.78 = (bf16[1024]{0:T(1024)(128)(2,1)S(1)}, bf16[2048,1024]{1,0:T(8,128)(2,1)S(1)}, f32[2048,1024]{1,0:T(8,128)}) fusion(f32[2048,1024]{1,0:T(8,128)} %fusion.91, f32[1024]{0:T(1024)S(1)} %convert_element_type.188, bf16[2048,1024]{1,0:T(8,128)(2,1)} %all-gather.10.cloned.1.call-done, bf16[1024,1024]{1,0:T(8,128)(2,1)S(1)} %copy-done), kind=kOutput, calls=%fused_computation.151 | convolution fusion | flops 4450155520 | bytes 27269120 | tf_op jit(solution)/shard_map/td,fd->tf/dot_general | solution.py:173
  260.0 6.2 convolution_convert_fusion.1
  266.3 10.4 %multiply_convert_fusion.2 = bf16[2048,1024]{1,0:T(8,128)(2,1)} fusion(f32[2048,1024]{1,0:T(8,128)} %get-tuple-element.31, f32[2048,1024]{1,0:T(8,128)} %fusion.91, f32[1024]{0:T(1024)S(1)} %convert_element_type.188), kind=kLoop, calls=%fused_computation.17 | loop fusion | flops 8388608 | bytes 20975616 | tf_op jit(solution)/shard_map/convert_element_type | solution.py:158
  276.7 8.4 %convolution_convert_fusion.2 = bf16[2048,1024]{1,0:T(8,128)(2,1)} fusion(bf16[2048,1024]{1,0:T(8,128)(2,1)} %multiply_convert_fusion.2, bf16[1024,1024]{1,0:T(8,128)(2,1)S(1)} %copy-done), kind=kOutput, calls=%fused_computation.43 | convolution fusion | flops 4297064448 | bytes 10485760 | tf_op jit(solution)/shard_map/dot_general | solution.py:162
  285.8 25.2 %reduce-scatter.9.cloned.1.call-done = bf16[512,1024]{1,0:T(8,128)(2,1)} async-done(((bf16[2048,1024]{1,0:T(8,128)(2,1)}), bf16[512,1024]{1,0:T(8,128)(2,1)}) %reduce-scatter.9.cloned.1.call-update) | async-done | bytes 1048592 | tf_op jit(solution)/shard_map/reduce_scatter | solution.py:178
  313.2 44.7 %reduce-scatter.7.cloned.1.call-done = bf16[512,1024]{1,0:T(8,128)(2,1)} async-done(((bf16[2048,1024]{1,0:T(8,128)(2,1)}), bf16[512,1024]{1,0:T(8,128)(2,1)}) %reduce-scatter.7.cloned.1.call-update) | async-done | bytes 1048592 | tf_op jit(solution)/shard_map/reduce_scatter | solution.py:161
  357.9 3.7 fusion.81
  364.4 9.5 %convolution_convert_fusion.6 = bf16[1024,1024]{1,0:T(8,128)(2,1)} fusion(bf16[2048,1024]{1,0:T(8,128)(2,1)} %all-gather.8.cloned.1.call-done, bf16[2048,1024]{1,0:T(8,128)(2,1)} %copy-done.55), kind=kOutput, calls=%fused_computation.90 | convolution fusion | flops 4296015872 | bytes 10485760 | tf_op jit(solution)/shard_map/td,tf->df/dot_general | solution.py:176
  373.9 5.9 convolution_convert_fusion.5
  379.9 19.1 %all-gather.12.cloned.1.call-done = bf16[2048,1024]{1,0:T(8,128)(2,1)} async-done(((bf16[512,1024]{1,0:T(8,128)(2,1)}), bf16[2048,1024]{1,0:T(8,128)(2,1)}) %all-gather.12.cloned.1.call-update) | async-done | bytes 4194320 | tf_op jit(solution)/shard_map/all_gather | solution.py:188
  398.9 4.5 convolution_convert_fusion.3
  410.4 5.9 fusion.42
  416.3 4.6 multiply_reduce_fusion.1
  429.6 14.7 %multiply_reduce_fusion = (f32[2,4,512]{2,1,0:T(4,128)S(1)}, f32[2,4,512,1024]{3,2,1,0:T(8,128)}) fusion(f32[2,4,512,1024]{3,2,1,0:T(8,128)} %copy-done.2, f32[2,4,512]{2,1,0:T(4,128)S(1)} %bitcast.140, bf16[2,512,4,64]{1,3,2,0:T(8,128)(2,1)} %copy.98, bf16[2,1024,4,64]{1,3,2,0:T(8,128)(2,1)S(1)} %copy-done.15), kind=kOutput, calls=%fused_computation.1 | convolution fusion | flops 549449728 | bytes 35160064 | tf_op jit(solution)/shard_map/rqhd,rkhd->rhqk/dot_general | solution.py:81
  444.3 7.8 fusion.90
  453.5 10.9 %multiply_convert_fusion = bf16[2,4,512,1024]{3,2,1,0:T(8,128)(2,1)} fusion(f32[2,4,512,1024]{3,2,1,0:T(8,128)} %get-tuple-element.54, f32[2,4,512,1024]{3,2,1,0:T(8,128)S(1)} %bitcast.125, f32[2,4,512]{2,1,0:T(4,128)S(1)} %get-tuple-element.53, f32[2,4,512]{2,1,0:T(4,128)S(1)} %bitcast.142), kind=kLoop, calls=%fused_computation | loop fusion | flops 16777216 | bytes 41975808 | tf_op jit(solution)/shard_map/convert_element_type | solution.py:85
  464.4 6.2 fusion.47
  497.4 23.2 %all-reduce.3 = (bf16[2,256]{1,0:T(2,128)(2,1)S(1)}, bf16[1024]{0:T(1024)(128)(2,1)S(1)}, bf16[1024]{0:T(1024)(128)(2,1)S(1)}, bf16[1024]{0:T(1024)(128)(2,1)S(1)}) all-reduce(bf16[2,256]{1,0:T(2,128)(2,1)S(1)} %pad_maximum_fusion.4, bf16[1024]{0:T(1024)(128)(2,1)S(1)} %reduce_sum.244, ...), channel_id=1, replica_groups=mesh['dp'=8,'mp'=4] {'dp'}, use_global_device_ids=true, to_apply=%region_21.22 | all-reduce | flops 3584 | bytes 14336 | tf_op jit(solution)/shard_map/psum | solution.py:216
  523.0 171.3 %all-reduce.7.cloned.1.call-done = (bf16[3,1024,256]{2,1,0:T(8,128)(2,1)}, bf16[256,1024]{1,0:T(8,128)(2,1)}, bf16[1024,1024]{1,0:T(8,128)(2,1)}, bf16[1024,1024]{1,0:T(8,128)(2,1)}) async-done(((bf16[3,1024,256]{2,1,0:T(8,128)(2,1)}, bf16[256,1024]{1,0:T(8,128)(2,1)}, bf16[1024,1024]{1,0:T(8,128)(2,1)}, bf16[1024,1024]{1,0:T(8,128)(2,1)}), (bf16[3,1024,256]{2,1,0:T(8,128)(2,1)}, ...) | async-done | bytes 6291472 | tf_op jit(solution)/shard_map/psum | solution.py:215
  705.3 35.1 %reduce-scatter.11.cloned.1.call-done = bf16[512,1024]{1,0:T(8,128)(2,1)} async-done(((bf16[2048,1024]{1,0:T(8,128)(2,1)}), bf16[512,1024]{1,0:T(8,128)(2,1)}) %reduce-scatter.11.cloned.1.call-update) | async-done | bytes 1048592 | tf_op jit(solution)/shard_map/reduce_scatter | solution.py:209
  745.0 39.5 %all-reduce.2 = (f32[2,1024]{1,0:T(2,128)}, f32[2,1024]{1,0:T(2,128)}) all-reduce(f32[2,1024]{1,0:T(2,128)S(1)} %get-tuple-element.59, f32[2,1024]{1,0:T(2,128)S(1)} %get-tuple-element.60), channel_id=1, replica_groups=mesh['dp'=8,'mp'=4] {'dp','mp'}, use_global_device_ids=true, to_apply=%region_33.34 | all-reduce | flops 4096 | bytes 32768 | tf_op jit(solution)/shard_map/psum | solution.py:224
  784.4 4.5 add_add_fusion.2
  (232 shorter events, 129.7 us)
Async XLA Ops:
  7.2 223.5 %copy-start = (bf16[1024,1024]{1,0:T(8,128)(2,1)S(1)}, bf16[1024,1024]{1,0:T(8,128)(2,1)}, u32[]{:S(2)}) copy-start(bf16[1024,1024]{1,0:T(8,128)(2,1)} %param.21) | copy-start | bytes 6291460
  7.2 14.5 %copy-start.48 = (bf16[2,256]{1,0:T(2,128)(2,1)S(1)}, bf16[2,256]{1,0:T(2,128)(2,1)}, u32[]{:S(2)}) copy-start(bf16[2,256]{1,0:T(2,128)(2,1)} %param.16) | copy-start | bytes 3076
  7.2 45.5 %all-gather.6.cloned.1.call-start = ((), (), s32[]{:S(2)}) async-start(), calls=%async_computation.4 | async-start | bytes 5242880 | tf_op jit(solution)/shard_map/all_gather | solution.py:135
  8.8 12.9 %copy-start.40 = (f32[512]{0:T(512)}, f32[512]{0:T(512)S(1)}, u32[]{:S(2)}) copy-start(f32[512]{0:T(512)S(1)} %broadcast_multiply_fusion.1) | copy-start | bytes 6148
  11.9 9.9 %copy-start.38 = (f32[1,1024]{1,0:T(1,128)}, f32[1,1024]{1,0:T(1,128)S(1)}, u32[]{:S(2)}) copy-start(f32[1,1024]{1,0:T(1,128)S(1)} %get-tuple-element.43) | copy-start | bytes 12292
  15.3 139.7 %reduce-scatter.5.cloned.1.call-start = ((), (), s32[]{:S(2)}) async-start(), calls=%async_computation.5 | async-start | bytes 5242880 | tf_op jit(solution)/shard_map/reduce_scatter | solution.py:147
  110.3 44.8 %copy-start.4 = (bf16[512,1024]{1,0:T(8,128)(2,1)S(1)}, bf16[512,1024]{1,0:T(8,128)(2,1)}, u32[]{:S(2)}) copy-start(bf16[512,1024]{1,0:T(8,128)(2,1)} %param.13) | copy-start | bytes 3145732
  110.3 84.5 %all-gather.8.cloned.1.call-start = ((), (), s32[]{:S(2)}) async-start(), calls=%async_computation.6 | async-start | bytes 5242880 | tf_op jit(solution)/shard_map/all_gather | solution.py:156
  160.2 70.5 %all-gather.10.cloned.1.call-start = ((), (), s32[]{:S(2)}) async-start(), calls=%async_computation.8 | async-start | bytes 5242880 | tf_op jit(solution)/shard_map/all_gather | solution.py:170
  160.8 150.2 %reduce-scatter.9.cloned.1.call-start = ((), (), s32[]{:S(2)}) async-start(), calls=%async_computation.9 | async-start | bytes 5242880 | tf_op jit(solution)/shard_map/reduce_scatter | solution.py:178
  230.7 29.2 %copy-start.54 = (bf16[1024,1024]{1,0:T(8,128)(2,1)S(1)}, bf16[1024,1024]{1,0:T(8,128)(2,1)}, u32[]{:S(2)}) copy-start(bf16[1024,1024]{1,0:T(8,128)(2,1)} %param.19) | copy-start | bytes 6291460
  266.2 91.7 %reduce-scatter.7.cloned.1.call-start = ((), (), s32[]{:S(2)}) async-start(), calls=%async_computation.7 | async-start | bytes 5242880 | tf_op jit(solution)/shard_map/reduce_scatter | solution.py:161
  285.1 25.9 %copy-start.7 = (bf16[512,1024]{1,0:T(8,128)(2,1)S(1)}, bf16[512,1024]{1,0:T(8,128)(2,1)}, u32[]{:S(2)}) copy-start(bf16[512,1024]{1,0:T(8,128)(2,1)} %reduce-scatter.5.cloned.1.call-done) | copy-start | bytes 3145732
  285.1 113.8 %all-gather.12.cloned.1.call-start = ((), (), s32[]{:S(2)}) async-start(), calls=%async_computation.10 | async-start | bytes 5242880 | tf_op jit(solution)/shard_map/all_gather | solution.py:188
  313.2 49.7 %copy-start.11 = (bf16[512,1024]{1,0:T(8,128)(2,1)S(1)}, bf16[512,1024]{1,0:T(8,128)(2,1)}, u32[]{:S(2)}) copy-start(bf16[512,1024]{1,0:T(8,128)(2,1)} %param.25) | copy-start | bytes 3145732
  364.3 329.9 %all-reduce.7.cloned.1.call-start = ((), (), s32[]{:S(2)}) async-start(), calls=%async_computation.12 | async-start | bytes 12582912 | tf_op jit(solution)/shard_map/psum | solution.py:215
  364.4 9.5 %copy-start.26 = (bf16[2048,1024]{1,0:T(8,128)(2,1)S(1)}, bf16[2048,1024]{1,0:T(8,128)(2,1)}, u32[]{:S(2)}) copy-start(bf16[2048,1024]{1,0:T(8,128)(2,1)} %all-gather.10.cloned.1.call-done) | copy-start | bytes 12582916
  364.4 9.5 %copy-start.28 = (bf16[2048,1024]{1,0:T(8,128)(2,1)S(1)}, bf16[2048,1024]{1,0:T(8,128)(2,1)}, u32[]{:S(2)}) copy-start(bf16[2048,1024]{1,0:T(8,128)(2,1)} %multiply_convert_fusion.2) | copy-start | bytes 12582916
  373.9 25.0 %copy-start.35 = (bf16[256,1024]{1,0:T(8,128)(2,1)S(1)}, bf16[256,1024]{1,0:T(8,128)(2,1)}, u32[]{:S(2)}) copy-start(bf16[256,1024]{1,0:T(8,128)(2,1)} %param.17) | copy-start | bytes 1572868
  410.4 10.5 %slice-start.4 = ((s8[8388608]{0:T(1024)(128)(4,1)}), s8[4194304]{0:T(1024)(128)(4,1)S(1)}, s32[]{:S(2)}) async-start(s8[8388608]{0:T(1024)(128)(4,1)} %bitcast.126), calls=%async_computation.17 | async-start | bytes 8388608
  429.6 14.7 %copy-start.20 = (bf16[2,512,4,64]{1,3,2,0:T(8,128)(2,1)S(1)}, bf16[2,512,4,64]{1,3,2,0:T(8,128)(2,1)}, u32[]{:S(2)}) copy-start(bf16[2,512,4,64]{1,3,2,0:T(8,128)(2,1)} %copy.98) | copy-start | bytes 1572868
  429.6 14.7 %copy-start.22 = (f32[2,512,4,64]{1,3,2,0:T(8,128)S(1)}, f32[2,512,4,64]{1,3,2,0:T(8,128)}, u32[]{:S(2)}) copy-start(f32[2,512,4,64]{1,3,2,0:T(8,128)} %fusion.42) | copy-start | bytes 3145732
  429.6 23.9 %slice-start = ((s8[16777216]{0:T(1024)(128)(4,1)}), s8[4194304]{0:T(1024)(128)(4,1)S(1)}, s32[]{:S(2)}) async-start(s8[16777216]{0:T(1024)(128)(4,1)} %bitcast.124), calls=%async_computation.13 | async-start | bytes 8388608
  429.6 23.9 %slice-start.1 = ((s8[16777216]{0:T(1024)(128)(4,1)}), s8[4194304]{0:T(1024)(128)(4,1)S(1)}, s32[]{:S(2)}) async-start(s8[16777216]{0:T(1024)(128)(4,1)} %bitcast.124), calls=%async_computation.14 | async-start | bytes 8388608
  429.6 23.9 %slice-start.2 = ((s8[16777216]{0:T(1024)(128)(4,1)}), s8[4194304]{0:T(1024)(128)(4,1)S(1)}, s32[]{:S(2)}) async-start(s8[16777216]{0:T(1024)(128)(4,1)} %bitcast.124), calls=%async_computation.15 | async-start | bytes 8388608
  453.5 21.8 %copy-start.23 = (bf16[32,8,2,1024]{3,1,2,0:T(8,128)(2,1)}, bf16[32,8,2,1024]{3,1,2,0:T(8,128)(2,1)S(1)}, u32[]{:S(2)}) copy-start(bf16[32,8,2,1024]{3,1,2,0:T(8,128)(2,1)S(1)} %copy.102) | copy-start | bytes 3145732
  483.0 257.4 %reduce-scatter.11.cloned.1.call-start = ((), (), s32[]{:S(2)}) async-start(), calls=%async_computation.11 | async-start | bytes 5242880 | tf_op jit(solution)/shard_map/reduce_scatter | solution.py:209
  702.3 38.1 %copy-start.39 = (f32[1,1024]{1,0:T(1,128)S(1)}, f32[1,1024]{1,0:T(1,128)}, u32[]{:S(2)}) copy-start(f32[1,1024]{1,0:T(1,128)} %copy-done.38) | copy-start | bytes 12292
  702.3 38.1 %copy-start.41 = (f32[512]{0:T(512)S(1)}, f32[512]{0:T(512)}, u32[]{:S(2)}) copy-start(f32[512]{0:T(512)} %copy-done.40) | copy-start | bytes 6148
  702.3 40.0 %copy-start.47 = (f32[512]{0:T(512)S(1)}, f32[512]{0:T(512)}, u32[]{:S(2)}) copy-start(f32[512]{0:T(512)} %copy-done.46) | copy-start | bytes 6148
  702.3 40.0 %copy-start.45 = (f32[512]{0:T(512)S(1)}, f32[512]{0:T(512)}, u32[]{:S(2)}) copy-start(f32[512]{0:T(512)} %copy-done.44) | copy-start | bytes 6148
  742.3 46.6 %copy-start.1 = (bf16[1024,1024]{1,0:T(8,128)(2,1)S(1)}, bf16[1024,1024]{1,0:T(8,128)(2,1)}, u32[]{:S(2)}) copy-start(bf16[1024,1024]{1,0:T(8,128)(2,1)} %param.21) | copy-start | bytes 6291460
  (39 other events, 131.2 us)
Sparse Core Ops, SparseCore 0:
  15.5 37.1 all-gather.5
  110.4 44.5 reduce-scatter.4
  160.3 34.4 all-gather.7
  196.2 34.4 all-gather.9
  266.3 44.5 reduce-scatter.8
  313.3 44.5 reduce-scatter.6
  364.4 34.4 all-gather.11
  483.1 211.0 all-reduce.6
  696.8 43.6 reduce-scatter.10
where the time goes:
time: 801 us; the launch traced here: 796 us
  waiting for transfers between devices  426 us (53%)
  matrix products  157 us (20%)
  other arithmetic  80 us (10%)
  blocking collectives  68.8 us (9%)
  local copies, waits for them, and re-layouts  47.7 us (6%)
  between operations  14.9 us (2%)
    psum x1, waiting for transfers between devices, shards(): lax.psum(grad_qkv.astype(jnp.bfloat16), 'dp').astype(jnp.float32)  171 us
    reduce_scatter x1, waiting for transfers between devices, shards(): lax.psum_scatter(jnp.dot(activ, w_down, preferred_element_type=jnp.float3...  44.7 us
    reduce_scatter x1, waiting for transfers between devices, shards(): lax.psum_scatter(jnp.dot(attended, w_out, preferred_element_type=jnp.floa...  44.1 us
    psum x1, blocking collectives, shards(): lax.psum((jnp.stack([grad_g1, grad_g2]), jnp.stack([grad_s1, grad_s2])),...  39.5 us
    reduce_scatter x1, waiting for transfers between devices, shards(): lax.psum_scatter(summed.astype(jnp.bfloat16), 'mp', scatter_dimension=0,...  35.1 us
    all_gather x1, waiting for transfers between devices, shards(): joined2 = lax.all_gather(lowered2, 'mp', axis=0, tiled=True)  34 us
    all_gather x1, waiting for transfers between devices, shards(): lax.all_gather(lowered, 'mp', axis=0, tiled=True)  27.5 us
    dot_general x1, matrix products, shards(): jnp.einsum('td,fd->tf', grad_z, w_down, preferred_element_type=jnp.float32)  27.2 us
  transfers between devices with their start and end apart: 9, of which 9 were waited for; matrix products, arithmetic and copies ran while one was open for 10% of the time, Pallas kernels for 0%

commit v1 on v0

--- a/solution.py
+++ b/solution.py
@@ -1,14 +1,210 @@
 import jax
 import jax.numpy as jnp
 from jax import lax
+from jax.experimental import pallas as pl
+from jax.experimental.pallas import tpu as pltpu
 from jax.sharding import PartitionSpec as P
 
 HD = 64
 LEN = 1024
 QBLK = 512
-
-
 EPS = 1e-05
+BLK = 256
+NEG = -1e30
+f32 = jnp.float32
+bf16 = jnp.bfloat16
+
+
+def nt(left, right):
+    return lax.dot_general(left, right, (((1,), (1,)), ((), ())), preferred_element_type=f32)
+
+
+def nn(left, right):
+    return lax.dot_general(left, right, (((1,), (0,)), ((), ())), preferred_element_type=f32)
+
+
+def tn(left, right):
+    return lax.dot_general(left, right, (((0,), (0,)), ((), ())), preferred_element_type=f32)
+
+
+def head_masks():
+    lane = lax.broadcasted_iota(jnp.int32, (BLK, 2 * HD), 1)
+    return (lane < HD, lane >= HD)
+
+
+def pick(mask, value):
+    return jnp.where(mask, value, jnp.zeros_like(value))
+
+
+def attn_fwd_body(info, q_ref, k_ref, v_ref, st_ref, o_ref, lse_ref):
+    block = pl.program_id(1)
+    query = q_ref[...]
+    first = st_ref[...]
+    q_pos = block * BLK + lax.broadcasted_iota(jnp.int32, (1, BLK), 1)
+    masks = head_masks()
+    sub = lax.broadcasted_iota(jnp.int32, (BLK, BLK), 0)
+
+    def step(at, carry):
+        j = block - at
+        row = pl.multiple_of((j ^ info[0]) * BLK, BLK)
+        keys = k_ref[pl.ds(row, BLK), :]
+        vals_t = v_ref[pl.ds(row, BLK), :].T
+        k_pos = sub + j * BLK
+        allowed = (k_pos >= first) & (k_pos <= q_pos)
+        out = []
+        for h in range(2):
+            top, total, acc = carry[h]
+            s = jnp.where(allowed, nt(pick(masks[h], keys), query), NEG)
+            new = jnp.maximum(top, jnp.max(s, axis=0, keepdims=True))
+            scale = jnp.exp(top - new)
+            p = jnp.exp(s - new)
+            total = total * scale + jnp.sum(p, axis=0, keepdims=True)
+            acc = acc * scale + nn(vals_t[h * HD : (h + 1) * HD], p.astype(bf16))
+            out.append((new, total, acc))
+        return tuple(out)
+
+    init = tuple(
+        (jnp.full((1, BLK), NEG, f32), jnp.zeros((1, BLK), f32), jnp.zeros((HD, BLK), f32))
+        for _ in range(2)
+    )
+    done = lax.fori_loop(0, block + 1 - info[1 + block], step, init)
+    both = jnp.concatenate([acc / total for _, total, acc in done], axis=0)
+    o_ref[...] = both.T.astype(bf16)
+    for h in range(2):
+        top, total, _ = done[h]
+        lse_ref[0, h : h + 1, :] = top + jnp.log(total)
+
+
+def attn_bwd_body(info, q_ref, k_ref, v_ref, st_ref, o_ref, lse_ref, do_ref, dq_ref, dk_ref, dv_ref, dk_acc, dv_acc):
+    block = pl.program_id(1)
+
+    @pl.when(block == 0)
+    def _():
+        dk_acc[...] = jnp.zeros_like(dk_acc)
+        dv_acc[...] = jnp.zeros_like(dv_acc)
+
+    query = q_ref[...]
+    cot = do_ref[...]
+    first = st_ref[...]
+    q_pos = block * BLK + lax.broadcasted_iota(jnp.int32, (1, BLK), 1)
+    masks = head_masks()
+    sub = lax.broadcasted_iota(jnp.int32, (BLK, BLK), 0)
+    prod_t = (cot.astype(f32) * o_ref[...].astype(f32)).T
+    delta = [jnp.sum(prod_t[h * HD : (h + 1) * HD], axis=0, keepdims=True) for h in range(2)]
+    lse = [lse_ref[0, h : h + 1, :] for h in range(2)]
+    q_heads = [pick(m, query) for m in masks]
+    c_heads = [pick(m, cot) for m in masks]
+
+    def step(j, dq):
+        row = pl.multiple_of((j ^ info[0]) * BLK, BLK)
+        keys = k_ref[pl.ds(row, BLK), :]
+        vals = v_ref[pl.ds(row, BLK), :]
+        k_pos = sub + j * BLK
+        allowed = (k_pos >= first) & (k_pos <= q_pos)
+        dk = dk_acc[pl.ds(row, BLK), :]
+        dv = dv_acc[pl.ds(row, BLK), :]
+        for h in range(2):
+            k_head = pick(masks[h], keys)
+            p = jnp.exp(jnp.where(allowed, nt(k_head, query) - lse[h], NEG))
+            dp = nt(pick(masks[h], vals), cot)
+            ds = (p * (dp - delta[h])).astype(bf16)
+            dv = dv + nn(p.astype(bf16), c_heads[h])
+            dk = dk + nn(ds, q_heads[h])
+            dq = dq + tn(ds, k_head)
+        dk_acc[pl.ds(row, BLK), :] = dk
+        dv_acc[pl.ds(row, BLK), :] = dv
+        return dq
+
+    dq = lax.fori_loop(info[1 + block], block + 1, step, jnp.zeros((BLK, 2 * HD), f32))
+    dq_ref[...] = (dq * HD**-0.5).astype(bf16)
+
+    @pl.when(block == pl.num_programs(1) - 1)
+    def _():
+        dk_ref[...] = dk_acc[...].astype(bf16)
+        dv_ref[...] = dv_acc[...].astype(bf16)
+
+
+def specs():
+    small = pl.BlockSpec((BLK, 2 * HD), lambda p, i, info: (i ^ info[0], p))
+    whole = pl.BlockSpec((LEN, 2 * HD), lambda p, i, info: (0, p))
+    start = pl.BlockSpec((1, BLK), lambda p, i, info: (0, i ^ info[0]))
+    lse = pl.BlockSpec((1, 2, BLK), lambda p, i, info: (p, 0, i ^ info[0]))
+    return small, whole, start, lse
+
+
+def attn_fwd(info, query, keys, values, start):
+    pairs = query.shape[1] // (2 * HD)
+    small, whole, first, lse = specs()
+    return pl.pallas_call(
+        attn_fwd_body,
+        out_shape=(
+            jax.ShapeDtypeStruct(query.shape, bf16),
+            jax.ShapeDtypeStruct((pairs, 2, LEN), f32),
+        ),
+        grid_spec=pltpu.PrefetchScalarGridSpec(
+            num_scalar_prefetch=1,
+            grid=(pairs, LEN // BLK),
+            in_specs=[small, whole, whole, first],
+            out_specs=[small, lse],
+        ),
+        cost_estimate=pl.CostEstimate(
+            flops=4 * pairs * 10 * BLK * BLK * 256 * 2, bytes_accessed=4 << 20, transcendentals=pairs * 20 * BLK * BLK
+        ),
+        name="attn_fwd",
+    )(info, query, keys, values, start)
+
+
+def attn_bwd(info, query, keys, values, start, out, lse, cot):
+    pairs = query.shape[1] // (2 * HD)
+    small, whole, first, lse_spec = specs()
+    shape = jax.ShapeDtypeStruct(query.shape, bf16)
+    return pl.pallas_call(
+        attn_bwd_body,
+        out_shape=(shape, shape, shape),
+        grid_spec=pltpu.PrefetchScalarGridSpec(
+            num_scalar_prefetch=1,
+            grid=(pairs, LEN // BLK),
+            in_specs=[small, whole, whole, first, small, lse_spec, small],
+            out_specs=[small, whole, whole],
+            scratch_shapes=[pltpu.VMEM((LEN, 2 * HD), f32), pltpu.VMEM((LEN, 2 * HD), f32)],
+        ),
+        cost_estimate=pl.CostEstimate(
+            flops=10 * pairs * 10 * BLK * BLK * 256 * 2, bytes_accessed=4 << 20, transcendentals=pairs * 20 * BLK * BLK
+        ),
+        name="attn_bwd",
+    )(info, query, keys, values, start, out, lse, cot)
+
+
+def up_body(a_ref, w_ref, b_ref, g_ref, s_ref):
+    rows = a_ref[...]
+    for part in range(w_ref.shape[1] // 256):
+        cols = slice(part * 256, part * 256 + 256)
+        u = nn(rows, w_ref[:, cols]) + b_ref[:, cols].astype(f32)
+        size = jnp.abs(u)
+        t = 1.0 / (1.0 + 0.3275911 * 0.7071067811865476 * size)
+        poly = t * (0.5 * 0.254829592 + t * (0.5 * -0.284496736 + t * (0.5 * 1.421413741 + t * (0.5 * -1.453152027 + t * (0.5 * 1.061405429)))))
+        bell = jnp.exp(-0.5 * u * u)
+        tail = poly * bell
+        cdf = jnp.where(u >= 0, 1.0 - tail, tail)
+        g_ref[:, cols] = (u * cdf).astype(bf16)
+        s_ref[:, cols] = (cdf + u * bell * 0.3989422804014327).astype(bf16)
+
+
+def up_gelu(rows, weight, bias):
+    m, k = rows.shape
+    n = weight.shape[1]
+    bm = 256
+    shape = jax.ShapeDtypeStruct((m, n), bf16)
+    tile = pl.BlockSpec((bm, n), lambda i: (i, 0))
+    return pl.pallas_call(
+        up_body,
+        out_shape=(shape, shape),
+        grid=(m // bm,),
+        in_specs=[pl.BlockSpec((bm, k), lambda i: (i, 0)), pl.BlockSpec((k, n), lambda i: (0, 0)), pl.BlockSpec((1, n), lambda i: (0, 0))],
+        out_specs=(tile, tile),
+        cost_estimate=pl.CostEstimate(flops=2 * m * n * k * 2, bytes_accessed=8 << 20, transcendentals=m * n),
+        name="up_gelu",
+    )(rows, weight, bias.reshape(1, n))
 
 
 def norm_rows(values, gain, shift):
@@ -110,7 +306,7 @@
     )
 
 
-def shards(
+def tensor_parallel_shards(
     tokens,
     segment_ids,
     w_qkv,
@@ -227,6 +423,234 @@
     return (block_out, grad_in) + tuple(weight_totals) + tuple(norm_totals)
 
 
+def row_per_chip(mesh):
+    return mesh.shape["mp"] == 4 and mesh.shape["dp"] == 8
+
+
+def swap(value, axis, size, bit):
+    return lax.ppermute(value, axis, [(i, i ^ bit) for i in range(size)])
+
+
+def core(value):
+    return swap(value, "mp", 4, 1)
+
+
+def cross(value):
+    return swap(value, "mp", 4, 2)
+
+
+def along(value, bit):
+    return swap(value, "dp", 8, bit)
+
+
+def after(value, *others):
+    return lax.optimization_barrier((value,) + others)[0]
+
+
+def take(value, at):
+    return lax.dynamic_index_in_dim(value, at, 0, keepdims=False)
+
+
+def place(whole, piece, at):
+    return lax.dynamic_update_index_in_dim(whole, piece, at, 0)
+
+
+def gather_spread(weight, ready):
+    me = lax.axis_index("dp") & 3
+    quarters = weight.reshape(4, weight.shape[0] // 4, weight.shape[1])
+    mine = take(quarters, me)
+    if ready is not None:
+        mine = after(mine, ready)
+    mine = cross(mine)
+    whole = jnp.zeros_like(quarters)
+    whole = place(whole, mine, me)
+    for bit in (1, 2, 3):
+        whole = place(whole, along(mine, bit), me ^ bit)
+    return whole.reshape(weight.shape)
+
+
+def reduce_all(own, other):
+    rows, cols = own.shape
+    me = lax.axis_index("dp")
+    side, deep = me & 1, me >> 1
+    eighth = rows // 8
+    own = own.reshape(2, 4, eighth, cols)
+    got = cross(other).reshape(2, 4, eighth, cols)
+    away = (take(own, 1 - side).astype(f32) + take(got, 1 - side).astype(f32)).astype(bf16)
+    near = along(away, 1)
+
+    def part(step):
+        at = deep ^ step
+        total = take(take(own, side), at).astype(f32) + take(take(got, side), at).astype(f32)
+        return total + take(near, at).astype(f32)
+
+    arrived = [along(part(step).astype(bf16), 2 * step) for step in (1, 2, 3)]
+    total = part(0)
+    for piece in arrived:
+        total = total + piece.astype(f32)
+    mine = lax.optimization_barrier(total.astype(bf16))
+    level = [mine] + [along(mine, 2 * step) for step in (1, 2, 3)]
+    return level, [along(piece, 1) for piece in level]
+
+
+def settle(whole, index, pieces):
+    me = lax.axis_index("dp")
+    side, deep = me & 1, me >> 1
+    zero = jnp.int32(0)
+    for flip in (0, 1):
+        for step in range(4):
+            piece = pieces[flip][step].astype(f32)[None, None, None]
+            whole = lax.dynamic_update_slice(
+                whole, piece, (jnp.int32(index), side ^ flip, deep ^ step, zero, zero)
+            )
+    return whole
+
+
+def reduce_weight(pairs):
+    rows, cols = pairs[0][0].shape
+    whole = jnp.zeros((len(pairs), 2, 4, rows // 8, cols), f32)
+    for index, (own, other) in enumerate(pairs):
+        whole = settle(whole, index, reduce_all(own, other))
+    return whole.reshape(len(pairs) * rows, cols)
+
+
+def row_per_chip_shards(
+    tokens,
+    segment_ids,
+    w_qkv,
+    b_qv,
+    w_out,
+    b_out,
+    w_up,
+    b_up,
+    w_down,
+    b_down,
+    ln_gain,
+    ln_bias,
+    out_grad,
+):
+    half = tokens.shape[0]
+    side = lax.axis_index("mp") & 1
+    resid = tokens.astype(f32)
+    normed, first_back = jax.vjp(norm_rows, resid, ln_gain[0], ln_bias[0])
+    a1_own = normed.astype(bf16)
+
+    qkv_other = cross(w_qkv)
+    small = cross(jnp.concatenate([b_qv.reshape(-1), b_up]))
+    out_other = cross(after(w_out, qkv_other))
+    up_other = gather_spread(w_up, qkv_other)
+    down_other = gather_spread(w_down, out_other)
+    width = b_qv.shape[1]
+    qv_biases = (b_qv.astype(f32), small[: 2 * width].reshape(2, width).astype(f32))
+    up_biases = (b_up, small[2 * width :])
+    qkvs, outs = (w_qkv, qkv_other), (w_out, out_other)
+    ups, downs = (w_up, up_other), (w_down, down_other)
+
+    a1 = jnp.concatenate([a1_own, core(a1_own)])
+    dz = jnp.concatenate([out_grad, core(out_grad)])
+    seg_other = core(segment_ids)
+    seg = jnp.concatenate([segment_ids, seg_other])
+    start = jnp.sum((seg[None, :] < seg[:, None]).astype(jnp.int32), axis=1)[None]
+    ordered = jnp.where(side == 0, seg, jnp.concatenate([seg_other, segment_ids]))
+    blocks = ordered.reshape(LEN // BLK, BLK)
+    low = jnp.sum((blocks[None, :, -1] < blocks[:, None, 0]).astype(jnp.int32), axis=1)
+    info = jnp.concatenate([(side * (LEN // BLK // 2))[None].astype(jnp.int32), low])
+
+    saved = []
+    for weight, bias in zip(qkvs, qv_biases):
+        query = (nn(a1, weight[0]) + bias[0]).astype(bf16) * jnp.bfloat16(HD**-0.5)
+        keys = nn(a1, weight[1]).astype(bf16)
+        values = (nn(a1, weight[2]) + bias[1]).astype(bf16)
+        out, lse = attn_fwd(info, query, keys, values, start)
+        saved.append((query, keys, values, out, lse))
+    outs_a = [entry[3] for entry in saved]
+
+    def pair_sum(lefts, rights, product):
+        there = sum(product(left[half:], right) for left, right in zip(lefts, rights))
+        came = core(there.astype(bf16))
+        here = sum(product(left[:half], right) for left, right in zip(lefts, rights))
+        return here + came.astype(f32)
+
+    mixed = resid + pair_sum(outs_a, outs, nn) + b_out.astype(f32)
+    normed2, second_back = jax.vjp(norm_rows, mixed, ln_gain[1], ln_bias[1])
+    a2_own = normed2.astype(bf16)
+    a2 = jnp.concatenate([a2_own, core(a2_own)])
+    acts = [up_gelu(a2, weight, bias) for weight, bias in zip(ups, up_biases)]
+    activs = [act[0] for act in acts]
+    grads_down = [tn(activ, dz).astype(bf16) for activ in activs]
+    dus = [(nt(dz, down) * act[1].astype(f32)).astype(bf16) for act, down in zip(acts, downs)]
+    grad_y = out_grad.astype(f32)
+    grad_n2 = pair_sum(dus, ups, nt)
+    grad_h, grad_g2, grad_s2 = second_back(grad_n2)
+    grad_h = grad_h + grad_y
+    dattn_own = grad_h.astype(bf16)
+    dattn = jnp.concatenate([dattn_own, core(dattn_own)])
+    grads_up = [tn(a2, du).astype(bf16) for du in dus]
+    block_out = (mixed + pair_sum(activs, downs, nn) + b_down.astype(f32)).astype(bf16)
+
+    grads_out, grads_qkv, sums, terms = [], [], [], []
+    for (query, keys, values, out, lse), weight, w_o, du in zip(saved, qkvs, outs, dus):
+        cot = nt(dattn, w_o).astype(bf16)
+        grads_out.append(tn(out, dattn).astype(bf16))
+        trio = attn_bwd(info, query, keys, values, start, out, lse, cot)
+        grads_qkv.append([tn(a1, piece).astype(bf16) for piece in trio])
+        terms.append(trio)
+        sums.append(
+            jnp.concatenate(
+                [jnp.sum(piece, axis=0, dtype=f32) for piece in (trio[0], trio[2], du)]
+            )
+        )
+    grad_n1 = pair_sum(
+        [piece for trio in terms for piece in trio],
+        [weight[i] for weight in qkvs for i in range(3)],
+        nt,
+    )
+    grad_x, grad_g1, grad_s1 = first_back(grad_n1)
+    grad_in = grad_x + grad_h
+
+    h = grads_down[0].shape[0] // 2
+    grad_down = reduce_weight([tuple(g[i * h : i * h + h] for g in grads_down) for i in range(2)])
+    grad_up = reduce_weight([tuple(g[i * h : i * h + h] for g in grads_up) for i in range(2)])
+    grad_wout = reduce_weight([tuple(grads_out)])
+    grad_qkv = reduce_weight([(grads_qkv[0][i], grads_qkv[1][i]) for i in range(3)])
+    grad_qkv = grad_qkv.reshape(w_qkv.shape)
+
+    common = jnp.concatenate(
+        [
+            jnp.sum(dattn_own, axis=0, dtype=f32),
+            jnp.sum(out_grad, axis=0, dtype=f32),
+            grad_g1,
+            grad_g2,
+            grad_s1,
+            grad_s2,
+        ]
+    )
+    common = common + core(common)
+    vector = jnp.concatenate([sums[0], common]) + cross(jnp.concatenate([sums[1], common]))
+    for bit in (1, 2, 4):
+        vector = vector + along(vector, bit)
+    wide, units = ln_gain.shape[1], b_up.shape[0]
+    ends = [2 * width, units, wide, wide, 2 * wide, 2 * wide]
+    cuts = [sum(ends[:i]) for i in range(len(ends) + 1)]
+    grad_bqv, grad_bup, grad_bout, grad_bdown, grad_gain, grad_shift = [
+        vector[low:high] for low, high in zip(cuts[:-1], cuts[1:])
+    ]
+    return (
+        block_out,
+        grad_in,
+        grad_qkv,
+        grad_bqv.reshape(b_qv.shape),
+        grad_wout,
+        grad_bout,
+        grad_up,
+        grad_bup,
+        grad_down,
+        grad_bdown,
+        grad_gain.reshape(ln_gain.shape),
+        grad_shift.reshape(ln_bias.shape),
+    )
+
+
 def solution(mesh):
     in_specs = (
         P(("dp", "mp"), None),
@@ -257,4 +681,5 @@
         P(),
         P(),
     )
-    return jax.shard_map(shards, mesh=mesh, in_specs=in_specs, out_specs=out_specs, check_vma=False)
+    body = row_per_chip_shards if row_per_chip(mesh) else tensor_parallel_shards
+    return jax.shard_map(body, mesh=mesh, in_specs=in_specs, out_specs=out_specs, check_vma=False)

time: 801 us -> 734 us (0.916)
  starting transfers between devices: 0.95 us -> 149 us
  waiting for transfers between devices: 426 us -> 299 us
  Pallas kernels: 0 us -> 78.3 us
  blocking collectives: 68.8 us -> 0 us
  matrix products: 157 us -> 113 us
  other arithmetic: 80 us -> 58 us
  local copies, waits for them, and re-layouts: 47.7 us -> 27.7 us
  between operations: 14.9 us -> 2.58 us
    ppermute x0 -> x121, waiting for transfers between devices: none -> 299 us  [swap(): return lax.ppermute(value, axis, [(i, i ^ bit) for i in range(size)])]
    psum x1 -> x0, waiting for transfers between devices: 171 us -> none  [shards(): lax.psum(grad_qkv.astype(jnp.bfloat16), 'dp').astype(jnp.float32)]
    ppermute x0 -> x121, starting transfers between devices: none -> 149 us  [swap(): return lax.ppermute(value, axis, [(i, i ^ bit) for i in range(size)])]
    reduce_scatter x4 -> x0, waiting for transfers between devices: 149 us -> none  [the longest x1 44.7 us: shards(): lax.psum_scatter(jnp.dot(activ, w_down, preferred_element_type=jnp.float3...]
    all_gather x4 -> x0, waiting for transfers between devices: 105 us -> none  [the longest x1 34 us: shards(): joined2 = lax.all_gather(lowered2, 'mp', axis=0, tiled=True)]
    pallas_call x0 -> x6, Pallas kernels: none -> 78.3 us  [the longest x2 32 us: attn_bwd(): pl.pallas_call(attn_bwd_body, out_shape=(shape, shape, shape), grid_spec=...]
    psum x2 -> x0, blocking collectives: 62.6 us -> none  [the longest x1 39.5 us: shards(): lax.psum((jnp.stack([grad_g1, grad_g2]), jnp.stack([grad_s1, grad_s2])),...]
    dot_general x30 -> x46, matrix products: 157 us -> 113 us  [the longest x20 46.7 us: nt(): lax.dot_general(left, right, (((1,), (1,)), ((), ())), preferred_element_...]
  transfers between devices with their start and end apart: 9 -> 121, of which waited for: 9 -> 62; matrix products, arithmetic and copies ran while one was open for 10% -> 18% of each run, Pallas kernels for 0% -> 4%
where the time goes in v1:
time: 734 us; the launch traced here: 728 us
  waiting for transfers between devices  299 us (41%)
  starting transfers between devices  149 us (20%)
  matrix products  113 us (15%)
  Pallas kernels  78.3 us (11%)
  other arithmetic  58 us (8%)
  local copies, waits for them, and re-layouts  27.7 us (4%)
    ppermute x121, waiting for transfers between devices, swap(): return lax.ppermute(value, axis, [(i, i ^ bit) for i in range(size)])  299 us
    ppermute x121, starting transfers between devices, swap(): return lax.ppermute(value, axis, [(i, i ^ bit) for i in range(size)])  149 us
    dot_general x20, matrix products, nt(): lax.dot_general(left, right, (((1,), (1,)), ((), ())), preferred_element_...  46.7 us
    dot_general x14, matrix products, nn(): lax.dot_general(left, right, (((1,), (0,)), ((), ())), preferred_element_...  37.3 us
    dynamic_update_slice x64, other arithmetic, settle(): lax.dynamic_update_slice(whole, piece, (jnp.int32(index), side ^ flip, de...  33.3 us
    pallas_call x2, Pallas kernels, attn_bwd(): pl.pallas_call(attn_bwd_body, out_shape=(shape, shape, shape), grid_spec=...  32 us
    dot_general x12, matrix products, tn(): lax.dot_general(left, right, (((0,), (0,)), ((), ())), preferred_element_...  29.4 us
    pallas_call x2, Pallas kernels, attn_fwd(): pl.pallas_call(attn_fwd_body, out_shape=(jax.ShapeDtypeStruct(query.shape...  27.8 us
  transfers between devices with their start and end apart: 121, of which 62 were waited for; matrix products, arithmetic and copies ran while one was open for 18% of the time, Pallas kernels for 4%

profile of v1, /device:TPU:0, one launch (start us, length us, event | category | flops | bytes accessed | tf_op | source)
XLA Modules:
  0.0 728.1 jit_solution(14759350710608418873)
XLA Ops:
  31.9 14.0 %attn_fwd.2 = (bf16[1024,256]{1,0:T(8,128)(2,1)}, f32[2,2,1024]{2,1,0:T(2,128)}) custom-call(s32[5]{0:T(128)} %pad_add_fusion.info, bf16[1024,256]{1,0:T(8,128)(2,1)} %fusion.18.q_ref, bf16[1024,256]{1,0:T(8,128)(2,1)} %convolution_convert_fusion.15.k_ref, bf16[1024,256]{1,0:T(8,128)(2,1)} %fusion.14.v_ref, s32[1,1024]{1,0:T(1,128)} %bitcast.559), custom_call_target="tpu_custom_call" | custom-call | flops 2684354560 | bytes 4194304 | tf_op jit(solution)/shard_map/attn_fwd/pallas_call | solution.py:138
  63.2 13.8 %attn_fwd.3 = (bf16[1024,256]{1,0:T(8,128)(2,1)}, f32[2,2,1024]{2,1,0:T(2,128)}) custom-call(s32[5]{0:T(128)} %pad_add_fusion.info, bf16[1024,256]{1,0:T(8,128)(2,1)} %fusion.17.q_ref, bf16[1024,256]{1,0:T(8,128)(2,1)} %convolution_convert_fusion.14.k_ref, bf16[1024,256]{1,0:T(8,128)(2,1)} %fusion.16.v_ref, s32[1,1024]{1,0:T(1,128)} %bitcast.560), custom_call_target="tpu_custom_call" | custom-call | flops 2684354560 | bytes 4194304 | tf_op jit(solution)/shard_map/attn_fwd/pallas_call | solution.py:138
  90.6 5.6 collective-permute-start.14
  96.5 13.9 %collective-permute-done.8 = bf16[256,1024]{1,0:T(8,128)(2,1)S(1)} collective-permute-done((bf16[256,1024]{1,0:T(8,128)(2,1)}, bf16[256,1024]{1,0:T(8,128)(2,1)S(1)}, u32[]{:S(2)}, u32[]{:S(2)}) %collective-permute-start.8) | collective-permute-done | bytes 524320 | tf_op jit(solution)/shard_map/ppermute | solution.py:431
  115.3 17.3 %collective-permute-done.12 = bf16[256,1024]{1,0:T(8,128)(2,1)S(1)} collective-permute-done((bf16[256,1024]{1,0:T(8,128)(2,1)S(1)}, bf16[256,1024]{1,0:T(8,128)(2,1)S(1)}, u32[]{:S(2)}, u32[]{:S(2)}) %collective-permute-start.12) | collective-permute-done | bytes 524320 | tf_op jit(solution)/shard_map/ppermute | solution.py:431
  137.5 9.2 %up_gelu.2 = (bf16[1024,1024]{1,0:T(8,128)(2,1)}, bf16[1024,1024]{1,0:T(8,128)(2,1)}) custom-call(bf16[1024,1024]{1,0:T(8,128)(2,1)} %pad_maximum_fusion.1.a_ref, bf16[1024,1024]{1,0:T(8,128)(2,1)} %w_ref.1, bf16[1,1024]{1,0:T(2,128)(2,1)} %reshape.522.b_ref), custom_call_target="tpu_custom_call" | custom-call | flops 4294967296 | bytes 8388608 | tf_op jit(solution)/shard_map/up_gelu/pallas_call | solution.py:199
  146.7 4.7 convert_reduce_fusion.1
  165.7 9.4 %up_gelu.3 = (bf16[1024,1024]{1,0:T(8,128)(2,1)}, bf16[1024,1024]{1,0:T(8,128)(2,1)}) custom-call(bf16[1024,1024]{1,0:T(8,128)(2,1)} %pad_maximum_fusion.1.a_ref, bf16[1024,1024]{1,0:T(8,128)(2,1)} %bitcast.509, bf16[1,1024]{1,0:T(2,128)(2,1)} %reshape.525.b_ref), custom_call_target="tpu_custom_call" | custom-call | flops 4294967296 | bytes 8388608 | tf_op jit(solution)/shard_map/up_gelu/pallas_call | solution.py:199
  175.1 4.8 convolution_convert_fusion
  199.9 14.8 %collective-permute-done.85 = bf16[512,1024]{1,0:T(8,128)(2,1)S(1)} collective-permute-done((bf16[512,1024]{1,0:T(8,128)(2,1)S(1)}, bf16[512,1024]{1,0:T(8,128)(2,1)S(1)}, u32[]{:S(2)}, u32[]{:S(2)}) %collective-permute-start.85) | collective-permute-done | bytes 1048608 | tf_op jit(solution)/shard_map/ppermute | solution.py:431
  215.0 22.3 %collective-permute-done.73 = bf16[512,1024]{1,0:T(8,128)(2,1)S(1)} collective-permute-done((bf16[512,1024]{1,0:T(8,128)(2,1)S(1)}, bf16[512,1024]{1,0:T(8,128)(2,1)S(1)}, u32[]{:S(2)}, u32[]{:S(2)}) %collective-permute-start.73) | collective-permute-done | bytes 1048608 | tf_op jit(solution)/shard_map/ppermute | solution.py:431
  238.9 20.8 %collective-permute-done.109 = bf16[512,1024]{1,0:T(8,128)(2,1)S(1)} collective-permute-done((bf16[512,1024]{1,0:T(8,128)(2,1)S(1)}, bf16[512,1024]{1,0:T(8,128)(2,1)S(1)}, u32[]{:S(2)}, u32[]{:S(2)}) %collective-permute-start.109) | collective-permute-done | bytes 1048608 | tf_op jit(solution)/shard_map/ppermute | solution.py:431
  261.4 19.4 %collective-permute-done.97 = bf16[512,1024]{1,0:T(8,128)(2,1)S(1)} collective-permute-done((bf16[512,1024]{1,0:T(8,128)(2,1)S(1)}, bf16[512,1024]{1,0:T(8,128)(2,1)S(1)}, u32[]{:S(2)}, u32[]{:S(2)}) %collective-permute-start.97) | collective-permute-done | bytes 1048608 | tf_op jit(solution)/shard_map/ppermute | solution.py:431
  298.8 6.4 collective-permute-done.98
  312.2 5.3 collective-permute-start.113
  317.5 6.1 collective-permute-start.112
  334.3 4.9 collective-permute-done.112
  355.2 8.1 %collective-permute-done.79 = bf16[64,1024]{1,0:T(8,128)(2,1)S(1)} collective-permute-done((bf16[64,1024]{1,0:T(8,128)(2,1)S(1)}, bf16[64,1024]{1,0:T(8,128)(2,1)S(1)}, u32[]{:S(2)}, u32[]{:S(2)}) %collective-permute-start.79) | collective-permute-done | bytes 131104 | tf_op jit(solution)/shard_map/ppermute | solution.py:431
  364.9 5.2 collective-permute-done.80
  370.2 4.9 collective-permute-done.102
  376.1 5.7 collective-permute-done.103
  389.7 5.1 collective-permute-done.81
  395.1 5.2 collective-permute-done.105
  405.6 5.1 collective-permute-done.83
  411.0 4.6 collective-permute-done.84
  416.0 5.0 collective-permute-done.106
  427.2 4.6 collective-permute-done.108
  467.7 16.0 %attn_bwd.2 = (bf16[1024,256]{1,0:T(8,128)(2,1)}, bf16[1024,256]{1,0:T(8,128)(2,1)}, bf16[1024,256]{1,0:T(8,128)(2,1)}) custom-call(s32[5]{0:T(128)} %pad_add_fusion.info, bf16[1024,256]{1,0:T(8,128)(2,1)} %fusion.18.q_ref, bf16[1024,256]{1,0:T(8,128)(2,1)} %convolution_convert_fusion.15.k_ref, bf16[1024,256]{1,0:T(8,128)(2,1)} %fusion.14.v_ref, ...), custom_call_target="tpu_custom_call" | custom-call | flops 6710886400 | bytes 4194304 | tf_op jit(solution)/shard_map/attn_bwd/pallas_call | solution.py:161
  502.6 16.0 %attn_bwd.3 = (bf16[1024,256]{1,0:T(8,128)(2,1)}, bf16[1024,256]{1,0:T(8,128)(2,1)}, bf16[1024,256]{1,0:T(8,128)(2,1)}) custom-call(s32[5]{0:T(128)} %pad_add_fusion.info, bf16[1024,256]{1,0:T(8,128)(2,1)} %fusion.17.q_ref, bf16[1024,256]{1,0:T(8,128)(2,1)} %convolution_convert_fusion.14.k_ref, bf16[1024,256]{1,0:T(8,128)(2,1)} %fusion.16.v_ref, ...), custom_call_target="tpu_custom_call" | custom-call | flops 6710886400 | bytes 4194304 | tf_op jit(solution)/shard_map/attn_bwd/pallas_call | solution.py:161
  556.1 4.7 collective-permute-done.45
  592.5 4.8 collective-permute-done.64
  663.8 4.6 collective-permute-done.38
  (577 shorter events, 433.4 us)
Async XLA Ops:
  11.5 40.1 %collective-permute-start.2 = (bf16[3,1024,256]{2,1,0:T(8,128)(2,1)}, bf16[3,1024,256]{2,1,0:T(8,128)(2,1)}, u32[]{:S(2)}, u32[]{:S(2)}) collective-permute-start(bf16[3,1024,256]{2,1,0:T(8,128)(2,1)} %param.15), channel_id=1, source_target_pairs={{0,2},{1,3},{2,0},{3,1},{4,6},{5,7},{6,4},{7,5},{8,10},{9,11},{10,... | collective-permute-start | bytes 4718600 | tf_op jit(solution)/shard_map/ppermute | solution.py:431
  51.6 25.4 %collective-permute-start.4 = (bf16[256,1024]{1,0:T(8,128)(2,1)}, bf16[256,1024]{1,0:T(8,128)(2,1)}, u32[]{:S(2)}, u32[]{:S(2)}) collective-permute-start(bf16[256,1024]{1,0:T(8,128)(2,1)} %param.17), channel_id=1, source_target_pairs={{0,2},{1,3},{2,0},{3,1},{4,6},{5,7},{6,4},{7,5},{8,10},{9,11},{10,... | collective-permute-start | bytes 1572872 | tf_op jit(solution)/shard_map/ppermute | solution.py:431
  53.6 27.8 %collective-permute-start.7 = (bf16[256,1024]{1,0:T(8,128)(2,1)}, bf16[256,1024]{1,0:T(8,128)(2,1)}, u32[]{:S(2)}, u32[]{:S(2)}) collective-permute-start(bf16[256,1024]{1,0:T(8,128)(2,1)} %dynamic-slice_bitcast_fusion.1), channel_id=1, source_target_pairs={{0,2},{1,3},{2,0},{3,1},{4,6},{5,7},{6,4},{7,5},{8,10},{9,11},{10,... | collective-permute-start | bytes 1572872 | tf_op jit(solution)/shard_map/ppermute | solution.py:431
  81.4 30.3 %collective-permute-start.5 = (bf16[512,1024]{1,0:T(8,128)(2,1)S(1)}, bf16[512,1024]{1,0:T(8,128)(2,1)S(1)}, u32[]{:S(2)}, u32[]{:S(2)}) collective-permute-start(bf16[512,1024]{1,0:T(8,128)(2,1)S(1)} %add_convert_fusion.5), channel_id=1, source_target_pairs={{0,1},{1,0},{2,3},{3,2},{4,5},{5,4},{6,7},{7,6},{8,9},{9,8},{10,11... | collective-permute-start | bytes 3145736 | tf_op jit(solution)/shard_map/ppermute | solution.py:431
  81.5 33.7 %collective-permute-start.10 = (bf16[256,1024]{1,0:T(8,128)(2,1)}, bf16[256,1024]{1,0:T(8,128)(2,1)S(1)}, u32[]{:S(2)}, u32[]{:S(2)}) collective-permute-start(bf16[256,1024]{1,0:T(8,128)(2,1)} %collective-permute-done.7), channel_id=1, source_target_pairs={{0,12},{4,8},{8,4},{12,0},{16,28},{20,24},{24,20},{28,16},{1,13},{... | collective-permute-start | bytes 1572872 | tf_op jit(solution)/shard_map/ppermute | solution.py:431
  85.5 29.7 %collective-permute-start.9 = (bf16[256,1024]{1,0:T(8,128)(2,1)}, bf16[256,1024]{1,0:T(8,128)(2,1)S(1)}, u32[]{:S(2)}, u32[]{:S(2)}) collective-permute-start(bf16[256,1024]{1,0:T(8,128)(2,1)} %collective-permute-done.7), channel_id=1, source_target_pairs={{0,8},{4,12},{8,0},{12,4},{16,24},{20,28},{24,16},{28,20},{1,9},{5... | collective-permute-start | bytes 1572872 | tf_op jit(solution)/shard_map/ppermute | solution.py:431
  87.4 23.1 %collective-permute-start.8 = (bf16[256,1024]{1,0:T(8,128)(2,1)}, bf16[256,1024]{1,0:T(8,128)(2,1)S(1)}, u32[]{:S(2)}, u32[]{:S(2)}) collective-permute-start(bf16[256,1024]{1,0:T(8,128)(2,1)} %collective-permute-done.7), channel_id=1, source_target_pairs={{0,4},{4,0},{8,12},{12,8},{16,20},{20,16},{24,28},{28,24},{1,5},{5... | collective-permute-start | bytes 1572872 | tf_op jit(solution)/shard_map/ppermute | solution.py:431
  90.6 43.0 %collective-permute-start.14 = (bf16[256,1024]{1,0:T(8,128)(2,1)S(1)}, bf16[256,1024]{1,0:T(8,128)(2,1)S(1)}, u32[]{:S(2)}, u32[]{:S(2)}) collective-permute-start(bf16[256,1024]{1,0:T(8,128)(2,1)S(1)} %collective-permute-done.11), channel_id=1, source_target_pairs={{0,12},{4,8},{8,4},{12,0},{16,28},{20,24},{24,20},{28,16},{1,13},{... | collective-permute-start | bytes 1572872 | tf_op jit(solution)/shard_map/ppermute | solution.py:431
  110.5 23.1 %collective-permute-start.13 = (bf16[256,1024]{1,0:T(8,128)(2,1)S(1)}, bf16[256,1024]{1,0:T(8,128)(2,1)S(1)}, u32[]{:S(2)}, u32[]{:S(2)}) collective-permute-start(bf16[256,1024]{1,0:T(8,128)(2,1)S(1)} %collective-permute-done.11), channel_id=1, source_target_pairs={{0,8},{4,12},{8,0},{12,4},{16,24},{20,28},{24,16},{28,20},{1,9},{5... | collective-permute-start | bytes 1572872 | tf_op jit(solution)/shard_map/ppermute | solution.py:431
  188.7 26.1 %collective-permute-start.85 = (bf16[512,1024]{1,0:T(8,128)(2,1)S(1)}, bf16[512,1024]{1,0:T(8,128)(2,1)S(1)}, u32[]{:S(2)}, u32[]{:S(2)}) collective-permute-start(bf16[512,1024]{1,0:T(8,128)(2,1)S(1)} %get-tuple-element.81), channel_id=1, source_target_pairs={{0,2},{1,3},{2,0},{3,1},{4,6},{5,7},{6,4},{7,5},{8,10},{9,11},{10,... | collective-permute-start | bytes 3145736 | tf_op jit(solution)/shard_map/ppermute | solution.py:431
  189.3 48.0 %collective-permute-start.73 = (bf16[512,1024]{1,0:T(8,128)(2,1)S(1)}, bf16[512,1024]{1,0:T(8,128)(2,1)S(1)}, u32[]{:S(2)}, u32[]{:S(2)}) collective-permute-start(bf16[512,1024]{1,0:T(8,128)(2,1)S(1)} %get-tuple-element.82), channel_id=1, source_target_pairs={{0,2},{1,3},{2,0},{3,1},{4,6},{5,7},{6,4},{7,5},{8,10},{9,11},{10,... | collective-permute-start | bytes 3145736 | tf_op jit(solution)/shard_map/ppermute | solution.py:431
  192.3 67.4 %collective-permute-start.109 = (bf16[512,1024]{1,0:T(8,128)(2,1)S(1)}, bf16[512,1024]{1,0:T(8,128)(2,1)S(1)}, u32[]{:S(2)}, u32[]{:S(2)}) collective-permute-start(bf16[512,1024]{1,0:T(8,128)(2,1)S(1)} %get-tuple-element.77), channel_id=1, source_target_pairs={{0,2},{1,3},{2,0},{3,1},{4,6},{5,7},{6,4},{7,5},{8,10},{9,11},{10,... | collective-permute-start | bytes 3145736 | tf_op jit(solution)/shard_map/ppermute | solution.py:431
  196.5 86.4 %collective-permute-start.17 = (bf16[512,1024]{1,0:T(8,128)(2,1)S(1)}, bf16[512,1024]{1,0:T(8,128)(2,1)S(1)}, u32[]{:S(2)}, u32[]{:S(2)}) collective-permute-start(bf16[512,1024]{1,0:T(8,128)(2,1)S(1)} %add_convert_fusion.1), channel_id=1, source_target_pairs={{0,1},{1,0},{2,3},{3,2},{4,5},{5,4},{6,7},{7,6},{8,9},{9,8},{10,11... | collective-permute-start | bytes 3145736 | tf_op jit(solution)/shard_map/ppermute | solution.py:431
  196.6 84.2 %collective-permute-start.97 = (bf16[512,1024]{1,0:T(8,128)(2,1)S(1)}, bf16[512,1024]{1,0:T(8,128)(2,1)S(1)}, u32[]{:S(2)}, u32[]{:S(2)}) collective-permute-start(bf16[512,1024]{1,0:T(8,128)(2,1)S(1)} %get-tuple-element.78), channel_id=1, source_target_pairs={{0,2},{1,3},{2,0},{3,1},{4,6},{5,7},{6,4},{7,5},{8,10},{9,11},{10,... | collective-permute-start | bytes 3145736 | tf_op jit(solution)/shard_map/ppermute | solution.py:431
  214.8 69.5 %collective-permute-start.15 = (bf16[512,1024]{1,0:T(8,128)(2,1)S(1)}, bf16[512,1024]{1,0:T(8,128)(2,1)S(1)}, u32[]{:S(2)}, u32[]{:S(2)}) collective-permute-start(bf16[512,1024]{1,0:T(8,128)(2,1)S(1)} %add_convert_fusion.3), channel_id=1, source_target_pairs={{0,1},{1,0},{2,3},{3,2},{4,5},{5,4},{6,7},{7,6},{8,9},{9,8},{10,11... | collective-permute-start | bytes 3145736 | tf_op jit(solution)/shard_map/ppermute | solution.py:431
  237.3 51.8 %collective-permute-start.86 = (bf16[4,64,1024]{2,1,0:T(8,128)(2,1)S(1)}, bf16[4,64,1024]{2,1,0:T(8,128)(2,1)S(1)}, u32[]{:S(2)}, u32[]{:S(2)}) collective-permute-start(bf16[4,64,1024]{2,1,0:T(8,128)(2,1)S(1)} %fusion.34), channel_id=1, source_target_pairs={{0,4},{4,0},{8,12},{12,8},{16,20},{20,16},{24,28},{28,24},{1,5},{5... | collective-permute-start | bytes 1572872 | tf_op jit(solution)/shard_map/ppermute | solution.py:431
  259.7 30.2 %collective-permute-start.74 = (bf16[4,64,1024]{2,1,0:T(8,128)(2,1)S(1)}, bf16[4,64,1024]{2,1,0:T(8,128)(2,1)S(1)}, u32[]{:S(2)}, u32[]{:S(2)}) collective-permute-start(bf16[4,64,1024]{2,1,0:T(8,128)(2,1)S(1)} %fusion.33), channel_id=1, source_target_pairs={{0,4},{4,0},{8,12},{12,8},{16,20},{20,16},{24,28},{28,24},{1,5},{5... | collective-permute-start | bytes 1572872 | tf_op jit(solution)/shard_map/ppermute | solution.py:431
  283.0 22.3 %collective-permute-start.98 = (bf16[4,64,1024]{2,1,0:T(8,128)(2,1)S(1)}, bf16[4,64,1024]{2,1,0:T(8,128)(2,1)S(1)}, u32[]{:S(2)}, u32[]{:S(2)}) collective-permute-start(bf16[4,64,1024]{2,1,0:T(8,128)(2,1)S(1)} %fusion.35), channel_id=1, source_target_pairs={{0,4},{4,0},{8,12},{12,8},{16,20},{20,16},{24,28},{28,24},{1,5},{5... | collective-permute-start | bytes 1572872 | tf_op jit(solution)/shard_map/ppermute | solution.py:431
  289.0 175.6 %collective-permute-start.18 = (bf16[512,1024]{1,0:T(8,128)(2,1)S(1)}, bf16[512,1024]{1,0:T(8,128)(2,1)S(1)}, u32[]{:S(2)}, u32[]{:S(2)}) collective-permute-start(bf16[512,1024]{1,0:T(8,128)(2,1)S(1)} %get-tuple-element.56), channel_id=1, source_target_pairs={{0,1},{1,0},{2,3},{3,2},{4,5},{5,4},{6,7},{7,6},{8,9},{9,8},{10,11... | collective-permute-start | bytes 3145736 | tf_op jit(solution)/shard_map/ppermute | solution.py:431
  317.5 21.7 %collective-permute-start.112 = (bf16[64,1024]{1,0:T(8,128)(2,1)S(1)}, bf16[64,1024]{1,0:T(8,128)(2,1)S(1)}, u32[]{:S(2)}, u32[]{:S(2)}) collective-permute-start(bf16[64,1024]{1,0:T(8,128)(2,1)S(1)} %get-tuple-element.65), channel_id=1, source_target_pairs={{0,16},{4,20},{8,24},{12,28},{16,0},{20,4},{24,8},{28,12},{1,17},{... | collective-permute-start | bytes 393224 | tf_op jit(solution)/shard_map/ppermute | solution.py:431
  339.2 100.8 %collective-permute-start.93 = (bf16[64,1024]{1,0:T(8,128)(2,1)S(1)}, bf16[64,1024]{1,0:T(8,128)(2,1)S(1)}, u32[]{:S(2)}, u32[]{:S(2)}) collective-permute-start(bf16[64,1024]{1,0:T(8,128)(2,1)S(1)} %fusion.91), channel_id=1, source_target_pairs={{0,4},{4,0},{8,12},{12,8},{16,20},{20,16},{24,28},{28,24},{1,5},{5... | collective-permute-start | bytes 393224 | tf_op jit(solution)/shard_map/ppermute | solution.py:431
  340.6 99.2 %collective-permute-start.92 = (bf16[64,1024]{1,0:T(8,128)(2,1)S(1)}, bf16[64,1024]{1,0:T(8,128)(2,1)S(1)}, u32[]{:S(2)}, u32[]{:S(2)}) collective-permute-start(bf16[64,1024]{1,0:T(8,128)(2,1)S(1)} %fusion.91), channel_id=1, source_target_pairs={{0,24},{4,28},{8,16},{12,20},{16,8},{20,12},{24,0},{28,4},{1,25},{... | collective-permute-start | bytes 393224 | tf_op jit(solution)/shard_map/ppermute | solution.py:431
  342.4 95.3 %collective-permute-start.91 = (bf16[64,1024]{1,0:T(8,128)(2,1)S(1)}, bf16[64,1024]{1,0:T(8,128)(2,1)S(1)}, u32[]{:S(2)}, u32[]{:S(2)}) collective-permute-start(bf16[64,1024]{1,0:T(8,128)(2,1)S(1)} %fusion.91), channel_id=1, source_target_pairs={{0,16},{4,20},{8,24},{12,28},{16,0},{20,4},{24,8},{28,12},{1,17},{... | collective-permute-start | bytes 393224 | tf_op jit(solution)/shard_map/ppermute | solution.py:431
  521.1 28.2 %collective-permute-start.44 = (bf16[1024,256]{1,0:T(8,128)(2,1)S(1)}, bf16[1024,256]{1,0:T(8,128)(2,1)S(1)}, u32[]{:S(2)}, u32[]{:S(2)}) collective-permute-start(bf16[1024,256]{1,0:T(8,128)(2,1)S(1)} %convolution_convert_fusion.6), channel_id=1, source_target_pairs={{0,2},{1,3},{2,0},{3,1},{4,6},{5,7},{6,4},{7,5},{8,10},{9,11},{10,... | collective-permute-start | bytes 1572872 | tf_op jit(solution)/shard_map/ppermute | solution.py:431
  524.8 28.8 %collective-permute-start.20 = (bf16[1024,256]{1,0:T(8,128)(2,1)S(1)}, bf16[1024,256]{1,0:T(8,128)(2,1)S(1)}, u32[]{:S(2)}, u32[]{:S(2)}) collective-permute-start(bf16[1024,256]{1,0:T(8,128)(2,1)S(1)} %convolution_convert_fusion.10), channel_id=1, source_target_pairs={{0,2},{1,3},{2,0},{3,1},{4,6},{5,7},{6,4},{7,5},{8,10},{9,11},{10,... | collective-permute-start | bytes 1572872 | tf_op jit(solution)/shard_map/ppermute | solution.py:431
  528.1 25.7 %collective-permute-start.32 = (bf16[1024,256]{1,0:T(8,128)(2,1)S(1)}, bf16[1024,256]{1,0:T(8,128)(2,1)S(1)}, u32[]{:S(2)}, u32[]{:S(2)}) collective-permute-start(bf16[1024,256]{1,0:T(8,128)(2,1)S(1)} %convolution_convert_fusion.8), channel_id=1, source_target_pairs={{0,2},{1,3},{2,0},{3,1},{4,6},{5,7},{6,4},{7,5},{8,10},{9,11},{10,... | collective-permute-start | bytes 1572872 | tf_op jit(solution)/shard_map/ppermute | solution.py:431
  530.2 25.7 %collective-permute-start.61 = (bf16[256,1024]{1,0:T(8,128)(2,1)S(1)}, bf16[256,1024]{1,0:T(8,128)(2,1)S(1)}, u32[]{:S(2)}, u32[]{:S(2)}) collective-permute-start(bf16[256,1024]{1,0:T(8,128)(2,1)S(1)} %convolution_convert_fusion.4), channel_id=1, source_target_pairs={{0,2},{1,3},{2,0},{3,1},{4,6},{5,7},{6,4},{7,5},{8,10},{9,11},{10,... | collective-permute-start | bytes 1572872 | tf_op jit(solution)/shard_map/ppermute | solution.py:431
  536.3 163.3 %collective-permute-start.19 = (bf16[512,1024]{1,0:T(8,128)(2,1)S(1)}, bf16[512,1024]{1,0:T(8,128)(2,1)S(1)}, u32[]{:S(2)}, u32[]{:S(2)}) collective-permute-start(bf16[512,1024]{1,0:T(8,128)(2,1)S(1)} %add_convert_fusion), channel_id=1, source_target_pairs={{0,1},{1,0},{2,3},{3,2},{4,5},{5,4},{6,7},{7,6},{8,9},{9,8},{10,11... | collective-permute-start | bytes 3145736 | tf_op jit(solution)/shard_map/ppermute | solution.py:431
  597.3 91.5 %collective-permute-start.51 = (bf16[128,256]{1,0:T(8,128)(2,1)S(1)}, bf16[128,256]{1,0:T(8,128)(2,1)S(1)}, u32[]{:S(2)}, u32[]{:S(2)}) collective-permute-start(bf16[128,256]{1,0:T(8,128)(2,1)S(1)} %fusion.131), channel_id=1, source_target_pairs={{0,24},{4,28},{8,16},{12,20},{16,8},{20,12},{24,0},{28,4},{1,25},{... | collective-permute-start | bytes 196616 | tf_op jit(solution)/shard_map/ppermute | solution.py:431
  602.2 87.9 %collective-permute-start.50 = (bf16[128,256]{1,0:T(8,128)(2,1)S(1)}, bf16[128,256]{1,0:T(8,128)(2,1)S(1)}, u32[]{:S(2)}, u32[]{:S(2)}) collective-permute-start(bf16[128,256]{1,0:T(8,128)(2,1)S(1)} %fusion.131), channel_id=1, source_target_pairs={{0,16},{4,20},{8,24},{12,28},{16,0},{20,4},{24,8},{28,12},{1,17},{... | collective-permute-start | bytes 196616 | tf_op jit(solution)/shard_map/ppermute | solution.py:431
  602.2 88.7 %collective-permute-start.49 = (bf16[128,256]{1,0:T(8,128)(2,1)S(1)}, bf16[128,256]{1,0:T(8,128)(2,1)S(1)}, u32[]{:S(2)}, u32[]{:S(2)}) collective-permute-start(bf16[128,256]{1,0:T(8,128)(2,1)S(1)} %fusion.131), channel_id=1, source_target_pairs={{0,8},{4,12},{8,0},{12,4},{16,24},{20,28},{24,16},{28,20},{1,9},{5... | collective-permute-start | bytes 196616 | tf_op jit(solution)/shard_map/ppermute | solution.py:431
  696.2 24.4 %collective-permute-start.72 = (bf16[32,1024]{1,0:T(8,128)(2,1)S(1)}, bf16[32,1024]{1,0:T(8,128)(2,1)S(1)}, u32[]{:S(2)}, u32[]{:S(2)}) collective-permute-start(bf16[32,1024]{1,0:T(8,128)(2,1)S(1)} %collective-permute-done.68), channel_id=1, source_target_pairs={{0,4},{4,0},{8,12},{12,8},{16,20},{20,16},{24,28},{28,24},{1,5},{5... | collective-permute-start | bytes 196616 | tf_op jit(solution)/shard_map/ppermute | solution.py:431
  (160 other events, 1715.3 us)
